TPU v7x, 32 devices: a whole 2x2x4 slice. The times are simulated.
32 devices in a mesh: span: 16 (over z, x, core), seq: 2 (over y).
Axes of the slice: x: 2, y: 2, z: 4, core: 2. Of those that a mesh axis runs over, the one named last changes fastest.
Arguments:
- tokens: bfloat16 [8192, 1024], P(('span', 'seq')), may hold values from -48 to 48
- w_qkv: bfloat16 [1024, 3072], P('span'), may hold values from -0.1875 to 0.1875
- w_out: bfloat16 [1024, 1024], replicated, may hold values from -0.1875 to 0.1875
- w_cross: bfloat16 [1024, 2048], replicated, may hold values from -0.1875 to 0.1875
- ln_gain: float32 [1024], replicated, may hold values from 0.5 to 1.5
- ln_bias: float32 [1024], replicated, may hold values from -3 to 3
- queries: bfloat16 [1024, 1024], replicated, may hold values from -144 to 144
Outputs:
- encoded: bfloat16 [8192, 1024], P(('span', 'seq'))
- cross_out: bfloat16 [1024, 1024], P('span')
All inputs are finite; a program needn't handle non-finite values.
Results may differ from a plain program's by a relative error of at most 0.013.
The roundings to bfloat16 on the way count: a program that leaves them out, or rounds other values in their place, can miss the bound.
Values may be sent and summed in bfloat16 or wider, within the bound.
A program may use at most 128 MiB of HBM per device.

v0:
```python
import jax
import jax.numpy as jnp
from jax import lax
from jax.sharding import PartitionSpec as P

H = 16
DH = 64
score_scale = 0.125


def layer_norm(residual, ln_gain, ln_bias):
    center = residual - jnp.mean(residual, -1, keepdims=True)
    spread = jnp.mean(center * center, -1, keepdims=True)
    return center * lax.rsqrt(spread + 1e-05) * ln_gain + ln_bias


def per_device(tokens, w_qkv, w_out, w_cross, ln_gain, ln_bias, queries):
    tok_rows = tokens.shape[0]
    model_width = tokens.shape[1]
    seq_count = lax.axis_size("seq")
    span_count = lax.axis_size("span")
    projected = jnp.dot(
        tokens,
        lax.all_gather(w_qkv, "span", axis=0, tiled=True),
        preferred_element_type=jnp.float32,
    )
    projected = projected.astype(jnp.bfloat16).reshape(tok_rows, 3, model_width)
    grouped = lax.all_to_all(projected, "seq", split_axis=2, concat_axis=0, tiled=True)
    span_length = tok_rows * seq_count
    heads_here = grouped.shape[2] // DH
    query_all = grouped[:, 0].reshape(span_length, heads_here, DH)
    key_all = grouped[:, 1].reshape(span_length, heads_here, DH)
    value_all = grouped[:, 2].reshape(span_length, heads_here, DH)
    block_rows = min(512, span_length)
    query_blocks = query_all.reshape(span_length // block_rows, block_rows, heads_here, DH)

    def attend(query_block):
        scores = (
            jnp.einsum("qhd,khd->hqk", query_block, key_all, preferred_element_type=jnp.float32)
            * score_scale
        )
        peaks = jnp.max(scores, -1, keepdims=True)
        powers = jnp.exp(scores - peaks)
        totals = jnp.sum(powers, -1, keepdims=True)
        mixed = jnp.einsum(
            "hqk,khd->qhd",
            powers.astype(jnp.bfloat16),
            value_all,
            preferred_element_type=jnp.float32,
        )
        mixed = mixed / jnp.transpose(totals, (1, 0, 2))
        return mixed.astype(jnp.bfloat16).reshape(block_rows, heads_here * DH)

    attn = lax.map(attend, query_blocks).reshape(span_length, heads_here * DH)
    attn_tokens = lax.all_to_all(attn, "seq", split_axis=0, concat_axis=1, tiled=True)
    residual = tokens.astype(jnp.float32) + jnp.dot(
        attn_tokens, w_out, preferred_element_type=jnp.float32
    )
    encoded = layer_norm(residual, ln_gain, ln_bias).astype(jnp.bfloat16)
    cross_kv = jnp.dot(encoded, w_cross, preferred_element_type=jnp.float32).astype(jnp.bfloat16)
    cross_keys = cross_kv[:, :model_width].reshape(tok_rows, H, DH)
    cross_values = cross_kv[:, model_width:].reshape(tok_rows, H, DH)
    query_count = queries.shape[0]
    query_heads = queries.reshape(query_count, H, DH)
    cross_scores = (
        jnp.einsum("qhd,khd->qhk", query_heads, cross_keys, preferred_element_type=jnp.float32)
        * score_scale
    )
    local_peak = jnp.max(cross_scores, -1)
    cross_peak = lax.pmax(local_peak, ("span", "seq"))
    cross_powers = jnp.exp(cross_scores - cross_peak[:, :, None])
    cross_total = jnp.sum(cross_powers, -1)
    numerator = jnp.einsum(
        "qhk,khd->qhd",
        cross_powers.astype(jnp.bfloat16),
        cross_values,
        preferred_element_type=jnp.float32,
    )
    numerator = numerator.reshape(query_count, model_width)
    own_rows = query_count // span_count
    summed, sum_total = lax.psum((numerator, cross_total), ("span", "seq"))
    row_start = lax.axis_index("span") * own_rows
    summed = lax.dynamic_slice_in_dim(summed, row_start, own_rows, 0)
    sum_total = lax.dynamic_slice_in_dim(sum_total, row_start, own_rows, 0)
    cross_out = summed.reshape(own_rows, H, DH) / sum_total[:, :, None]
    return (encoded, cross_out.reshape(own_rows, model_width).astype(jnp.bfloat16))


def solution(mesh):
    in_specs = (P(("span", "seq"), None), P("span", None), P(), P(), P(), P(), P())
    out_specs = (P(("span", "seq"), None), P("span", None))
    return jax.shard_map(
        per_device, mesh=mesh, in_specs=in_specs, out_specs=out_specs, check_vma=False
    )
```

profile of v0, /device:TPU:0, one launch (start us, length us, event | category | flops | bytes accessed | tf_op | source)
XLA Modules:
  0.0 455.3 jit_solution(16979895533489003373)
XLA Ops:
  7.2 0.0 copy-start
  7.2 0.0 all-gather.2.cloned.1.call-start
  7.2 0.7 all-gather.2.cloned.1.call-update
  7.9 66.5 %all-gather.2.cloned.1.call-done = bf16[1024,3072]{1,0:T(8,128)(2,1)} async-done(((bf16[64,3072]{1,0:T(8,128)(2,1)}), bf16[1024,3072]{1,0:T(8,128)(2,1)}) %all-gather.2.cloned.1.call-update) | async-done | bytes 6291472 | tf_op jit(solution)/shard_map/all_gather | solution.py:24
  74.4 5.9 %convolution_convert_fusion = bf16[256,3072]{1,0:T(8,128)(2,1)} fusion(bf16[256,1024]{1,0:T(8,128)(2,1)} %param.7, bf16[1024,3072]{1,0:T(8,128)(2,1)} %all-gather.2.cloned.1.call-done), kind=kOutput, calls=%fused_computation.15 | convolution fusion | flops 1611399168 | bytes 8388608 | tf_op jit(solution)/shard_map/dot_general | solution.py:22
  80.3 2.6 copy.36
  82.9 2.8 copy.37
  85.7 28.1 %all_to_all.37 = bf16[256,3,1024]{0,1,2:T(4,128)(2,1)S(1)} all-to-all(bf16[256,3,1024]{0,1,2:T(4,128)(2,1)S(1)} %copy.37), channel_id=1, replica_groups=mesh['span'=16,'seq'=2] {'seq'}, dimensions={2} | all-to-all | bytes 3145728 | tf_op jit(solution)/shard_map/all_to_all | solution.py:28
  113.8 1.4 copy.38
  115.1 2.6 copy.39
  117.8 2.3 fusion.20
  120.0 1.0 copy.40
  121.0 0.2 copy.41
  121.2 1.3 copy.42
  122.5 0.0 copy-start.3
  122.5 1.3 multiply_reduce_fusion
  123.8 1.4 fusion.7
  125.2 0.0 copy-done.3
  125.2 0.0 copy-start.1
  125.2 2.4 divide_convert_fusion
  127.6 0.0 copy-start.5
  127.6 0.0 copy-start.6
  127.6 1.2 all_to_all.31
  128.8 0.9 copy.44
  129.7 3.5 all-to-all-start.1
  133.2 0.2 all-reduce.4.cloned.1.call-start
  133.4 4.0 copy.47
  137.4 3.6 all-to-all-done.1
  141.0 0.0 copy-done
  141.0 0.0 copy-done.1
  141.0 0.8 fusion.22
  141.8 0.3 multiply_reduce_fusion.1
  142.1 0.0 copy-done.5
  142.1 0.0 copy-done.6
  142.1 0.2 add_convert_fusion
  142.3 0.0 copy-start.2
  142.4 3.7 convolution_convert_fusion.1
  146.0 0.9 fusion.21
  146.9 0.0 copy-done.2
  146.9 1.2 copy.46
  148.1 10.3 %bitcast_reduce_fusion = (f32[1024,16]{0,1:T(8,128)}, f32[16,256,1024]{2,1,0:T(8,128)}) fusion(bf16[256,16,64]{0,2,1:T(8,128)(2,1)S(1)} %bitcast.58, bf16[1024,16,64]{0,2,1:T(8,128)(2,1)} %bitcast.51), kind=kOutput, calls=%fused_computation.1 | convolution fusion | flops 545243136 | bytes 19464192 | tf_op jit(solution)/shard_map/qhd,khd->qhk/dot_general | solution.py:66
  158.4 0.0 all-reduce.4.cloned.1.call-update
  158.5 0.0 all-reduce.6.cloned.1.call-start
  158.5 0.2 copy.45
  158.7 117.2 %all-reduce.4.cloned.1.call-done = f32[1024,16]{0,1:T(8,128)} async-done(((f32[1024,16]{0,1:T(8,128)}), f32[1024,16]{0,1:T(8,128)}) %all-reduce.4.cloned.1.call-update) | async-done | bytes 65552 | tf_op jit(solution)/shard_map/pmax | solution.py:70
  276.0 10.7 %fusion.3 = f32[16,64,1024]{2,1,0:T(8,128)} fusion(bf16[256,16,64]{0,2,1:T(8,128)(2,1)S(1)} %bitcast.59, f32[16,256,1024]{2,1,0:T(8,128)} %get-tuple-element.29, f32[1024,16]{0,1:T(8,128)} %all-reduce.4.cloned.1.call-done), kind=kOutput, calls=%fused_computation.5 | convolution fusion | flops 549453824 | bytes 21561344 | tf_op jit(solution)/shard_map/qhk,khd->qhd/dot_general | solution.py:73
  286.6 0.0 copy-start.4
  286.6 5.4 %copy.49 = f32[1024,1024]{1,0:T(8,128)} copy(f32[1024,1024]{0,1:T(8,128)} %bitcast.50) | data formatting | bytes 8388608 | tf_op jit(solution)/shard_map/reshape | solution.py:79
  292.0 0.0 copy-done.4
  292.0 9.3 %fusion.1 = f32[1024,16]{0,1:T(8,128)} fusion(f32[16,256,1024]{2,1,0:T(8,128)} %get-tuple-element.29, f32[1024,16]{0,1:T(8,128)S(1)} %copy-done.4), kind=kLoop, calls=%fused_computation.3 | loop fusion | flops 12566528 | bytes 16908288 | tf_op jit(solution)/shard_map/reduce_sum | solution.py:72
  301.3 0.0 all-reduce.6.cloned.1.call-update
  301.3 144.6 %all-reduce.6.cloned.1.call-done = (f32[1024,16]{0,1:T(8,128)}, f32[1024,1024]{1,0:T(8,128)}) async-done(((f32[1024,16]{0,1:T(8,128)}, f32[1024,1024]{1,0:T(8,128)}), (f32[1024,16]{0,1:T(8,128)}, f32[1024,1024]{1,0:T(8,128)})) %all-reduce.6.cloned.1.call-update) | async-done | bytes 4259856 | tf_op jit(solution)/shard_map/psum | solution.py:81
  445.9 0.8 constant_dynamic-slice_fusion
  446.7 0.1 copy.50
  446.7 0.2 div.36
  446.9 0.2 div.37
  447.1 1.7 divide_convert_fusion.1
  (2 shorter events, 0.0 us)
Async XLA Ops:
  7.2 133.8 %copy-start = (bf16[1024,1024]{1,0:T(8,128)(2,1)S(1)}, bf16[1024,1024]{1,0:T(8,128)(2,1)}, u32[]{:S(2)}) copy-start(bf16[1024,1024]{1,0:T(8,128)(2,1)} %param.9) | copy-start | bytes 6291460
  7.2 67.2 %all-gather.2.cloned.1.call-start = ((), (), s32[]{:S(2)}) async-start(), calls=%async_computation.2 | async-start | bytes 6684672 | tf_op jit(solution)/shard_map/all_gather | solution.py:24
  122.5 2.7 copy-start.3
  125.2 15.8 %copy-start.1 = (bf16[256,1024]{1,0:T(8,128)(2,1)S(1)}, bf16[256,1024]{1,0:T(8,128)(2,1)}, u32[]{:S(2)}) copy-start(bf16[256,1024]{1,0:T(8,128)(2,1)} %param.7) | copy-start | bytes 1572868
  127.6 14.5 %copy-start.5 = (f32[1024]{0:T(1024)S(1)}, f32[1024]{0:T(1024)}, u32[]{:S(2)}) copy-start(f32[1024]{0:T(1024)} %param.12) | copy-start | bytes 12292
  127.6 14.5 %copy-start.6 = (f32[1024]{0:T(1024)S(1)}, f32[1024]{0:T(1024)}, u32[]{:S(2)}) copy-start(f32[1024]{0:T(1024)} %param.11) | copy-start | bytes 12292
  129.7 11.3 %all-to-all-start.1 = ((bf16[2,256,512]{1,2,0:T(8,128)(2,1)}), bf16[2,256,512]{1,2,0:T(8,128)(2,1)S(1)}, u32[]{:S(2)}, u32[]{:S(2)}) async-start(bf16[2,256,512]{1,2,0:T(8,128)(2,1)} %copy.44), calls=%async_computation.1 | async-start | bytes 1048576 | tf_op jit(solution)/shard_map/all_to_all | solution.py:55
  133.2 142.8 %all-reduce.4.cloned.1.call-start = ((), (), s32[]{:S(2)}) async-start(), calls=%async_computation.3 | async-start | bytes 131072 | tf_op jit(solution)/shard_map/pmax | solution.py:70
  142.3 4.5 copy-start.2
  158.5 287.4 %all-reduce.6.cloned.1.call-start = ((), (), s32[]{:S(2)}) async-start(), calls=%async_computation.4 | async-start | bytes 8519680 | tf_op jit(solution)/shard_map/psum | solution.py:81
  286.6 5.4 %copy-start.4 = (f32[1024,16]{0,1:T(8,128)S(1)}, f32[1024,16]{0,1:T(8,128)}, u32[]{:S(2)}) copy-start(f32[1024,16]{0,1:T(8,128)} %all-reduce.4.cloned.1.call-done) | copy-start | bytes 196612
Sparse Core Ops, SparseCore 0:
  10.3 64.1 all-gather.1
  158.6 117.3 all-reduce.3
  301.4 144.3 all-reduce.5
where the time goes:
time: 456 us; the launch traced here: 455 us
  waiting for transfers between devices  333 us (73%)
  matrix products  35.1 us (8%)
  local copies, waits for them, and re-layouts  29 us (6%)
  blocking collectives  28.1 us (6%)
  between operations  13.9 us (3%)
  other arithmetic  12.8 us (3%)
    psum x1, waiting for transfers between devices, per_device(): summed, sum_total = lax.psum((numerator, cross_total), ('span', 'seq'))  145 us
    pmax x1, waiting for transfers between devices, per_device(): cross_peak = lax.pmax(local_peak, ('span', 'seq'))  117 us
    all_gather x1, waiting for transfers between devices, per_device(): lax.all_gather(w_qkv, 'span', axis=0, tiled=True)  66.5 us
    all_to_all x1, blocking collectives, per_device(): lax.all_to_all(projected, 'seq', split_axis=2, concat_axis=0, tiled=True)  28.1 us
    dot_general x1, matrix products, per_device(): jnp.einsum('qhk,khd->qhd', cross_powers.astype(jnp.bfloat16), cross_value...  10.7 us
    dot_general x1, matrix products, per_device(): jnp.einsum('qhd,khd->qhk', query_heads, cross_keys, preferred_element_typ...  10.3 us
    reduce_sum x1, other arithmetic, per_device(): cross_total = jnp.sum(cross_powers, -1)  9.28 us
  transfers between devices with their start and end apart: 4, of which 4 were waited for; matrix products, arithmetic and copies ran while one was open for 1% of the time, Pallas kernels for 0%

commit v1 on v0

--- a/solution.py
+++ b/solution.py
@@ -6,6 +6,19 @@
 H = 16
 DH = 64
 score_scale = 0.125
+
+
+def collect(x, axis, dim):
+    ways = lax.axis_size(axis)
+    up = [(d, (d + 1) % ways) for d in range(ways)]
+    down = [(d, (d - 1) % ways) for d in range(ways)]
+    earlier, later = ([x], [x])
+    for _ in range(ways // 2):
+        earlier.append(lax.ppermute(earlier[-1], axis, up))
+    for _ in range((ways - 1) // 2):
+        later.append(lax.ppermute(later[-1], axis, down))
+    line = jnp.concatenate([*earlier[::-1], *later[1:]], axis=dim)
+    return jnp.roll(line, (lax.axis_index(axis) - ways // 2) * x.shape[dim], axis=dim)
 
 
 def layer_norm(residual, ln_gain, ln_bias):
@@ -19,11 +32,7 @@
     model_width = tokens.shape[1]
     seq_count = lax.axis_size("seq")
     span_count = lax.axis_size("span")
-    projected = jnp.dot(
-        tokens,
-        lax.all_gather(w_qkv, "span", axis=0, tiled=True),
-        preferred_element_type=jnp.float32,
-    )
+    projected = jnp.dot(tokens, collect(w_qkv, "span", 0), preferred_element_type=jnp.float32)
     projected = projected.astype(jnp.bfloat16).reshape(tok_rows, 3, model_width)
     grouped = lax.all_to_all(projected, "seq", split_axis=2, concat_axis=0, tiled=True)
     span_length = tok_rows * seq_count

time: 456 us -> 478 us (1.048)
  starting transfers between devices: 3.79 us -> 38.1 us
  waiting for transfers between devices: 333 us -> 309 us
  local copies, waits for them, and re-layouts: 29 us -> 43.2 us
    all_gather x1 -> x0, waiting for transfers between devices: 66.5 us -> none  [per_device(): lax.all_gather(w_qkv, 'span', axis=0, tiled=True)]
    ppermute x0 -> x15, waiting for transfers between devices: none -> 46.4 us  [the longest x8 46 us: collect(): earlier.append(lax.ppermute(earlier[-1], axis, up))]
    ppermute x0 -> x15, starting transfers between devices: none -> 34.3 us  [the longest x7 30.9 us: collect(): later.append(lax.ppermute(later[-1], axis, down))]
    unnamed x15 -> x80, local copies, waits for them, and re-layouts: 4 us -> 22.6 us
  transfers between devices with their start and end apart: 4 -> 18, of which waited for: 4 -> 12; matrix products, arithmetic and copies ran while one was open for 1% -> 4% of each run, Pallas kernels for 0% -> 0%
where the time goes in v1:
time: 478 us; the launch traced here: 477 us
  waiting for transfers between devices  309 us (65%)
  local copies, waits for them, and re-layouts  43.2 us (9%)
  starting transfers between devices  38.1 us (8%)
  matrix products  31.1 us (7%)
  blocking collectives  27.8 us (6%)
  between operations  14.5 us (3%)
  other arithmetic  12.8 us (3%)
    psum x1, waiting for transfers between devices, per_device(): summed, sum_total = lax.psum((numerator, cross_total), ('span', 'seq'))  145 us
    pmax x1, waiting for transfers between devices, per_device(): cross_peak = lax.pmax(local_peak, ('span', 'seq'))  115 us
    ppermute x8, waiting for transfers between devices, collect(): earlier.append(lax.ppermute(earlier[-1], axis, up))  46 us
    ppermute x7, starting transfers between devices, collect(): later.append(lax.ppermute(later[-1], axis, down))  30.9 us
    all_to_all x1, blocking collectives, per_device(): lax.all_to_all(projected, 'seq', split_axis=2, concat_axis=0, tiled=True)  27.8 us
    unnamed x80, local copies, waits for them, and re-layouts  22.6 us
    dot_general x1, matrix products, per_device(): jnp.einsum('qhk,khd->qhd', cross_powers.astype(jnp.bfloat16), cross_value...  10.8 us
    dot_general x1, matrix products, per_device(): jnp.einsum('qhd,khd->qhk', query_heads, cross_keys, preferred_element_typ...  10.3 us
  transfers between devices with their start and end apart: 18, of which 12 were waited for; matrix products, arithmetic and copies ran while one was open for 4% of the time, Pallas kernels for 0%

profile of v1, /device:TPU:0, one launch (start us, length us, event | category | flops | bytes accessed | tf_op | source)
XLA Modules:
  0.0 476.9 jit_solution(130620742023209305)
XLA Ops:
  7.2 0.5 collective-permute-start
  7.7 10.6 %collective-permute-done = bf16[64,3072]{1,0:T(8,128)(2,1)S(1)} collective-permute-done((bf16[64,3072]{1,0:T(8,128)(2,1)}, bf16[64,3072]{1,0:T(8,128)(2,1)S(1)}, u32[]{:S(2)}, u32[]{:S(2)}) %collective-permute-start) | collective-permute-done | bytes 393248 | tf_op jit(solution)/shard_map/ppermute | solution.py:17
  18.4 4.4 collective-permute-start.8
  22.8 5.6 %collective-permute-done.1 = bf16[64,3072]{1,0:T(8,128)(2,1)S(1)} collective-permute-done((bf16[64,3072]{1,0:T(8,128)(2,1)S(1)}, bf16[64,3072]{1,0:T(8,128)(2,1)S(1)}, u32[]{:S(2)}, u32[]{:S(2)}) %collective-permute-start.1) | collective-permute-done | bytes 393248 | tf_op jit(solution)/shard_map/ppermute | solution.py:17
  28.4 4.6 collective-permute-start.9
  33.0 5.3 %collective-permute-done.2 = bf16[64,3072]{1,0:T(8,128)(2,1)S(1)} collective-permute-done((bf16[64,3072]{1,0:T(8,128)(2,1)S(1)}, bf16[64,3072]{1,0:T(8,128)(2,1)S(1)}, u32[]{:S(2)}, u32[]{:S(2)}) %collective-permute-start.2) | collective-permute-done | bytes 393248 | tf_op jit(solution)/shard_map/ppermute | solution.py:17
  38.4 4.6 collective-permute-start.10
  43.0 5.3 %collective-permute-done.3 = bf16[64,3072]{1,0:T(8,128)(2,1)S(1)} collective-permute-done((bf16[64,3072]{1,0:T(8,128)(2,1)S(1)}, bf16[64,3072]{1,0:T(8,128)(2,1)S(1)}, u32[]{:S(2)}, u32[]{:S(2)}) %collective-permute-start.3) | collective-permute-done | bytes 393248 | tf_op jit(solution)/shard_map/ppermute | solution.py:17
  48.4 0.4 collective-permute-start.4
  48.8 4.2 collective-permute-start.11
  53.0 5.4 %collective-permute-done.4 = bf16[64,3072]{1,0:T(8,128)(2,1)S(1)} collective-permute-done((bf16[64,3072]{1,0:T(8,128)(2,1)S(1)}, bf16[64,3072]{1,0:T(8,128)(2,1)S(1)}, u32[]{:S(2)}, u32[]{:S(2)}) %collective-permute-start.4) | collective-permute-done | bytes 393248 | tf_op jit(solution)/shard_map/ppermute | solution.py:17
  58.4 1.1 collective-permute-start.5
  59.5 0.8 copy-done.10
  60.3 3.5 collective-permute-start.12
  63.8 4.6 collective-permute-done.5
  68.4 0.7 collective-permute-start.6
  69.1 4.8 %collective-permute-start.13 = (bf16[64,3072]{1,0:T(8,128)(2,1)}, bf16[64,3072]{1,0:T(8,128)(2,1)}, u32[]{:S(2)}, u32[]{:S(2)}) collective-permute-start(bf16[64,3072]{1,0:T(8,128)(2,1)} %collective-permute-done.12), channel_id=1, source_target_pairs={{0,30},{2,0},{4,2},{6,4},{8,6},{10,8},{12,10},{14,12},{16,14},{18,... | collective-permute-start | bytes 1179656 | tf_op jit(solution)/shard_map/ppermute | solution.py:19
  73.9 4.6 collective-permute-done.6
  78.5 0.6 collective-permute-start.7
  79.5 4.7 collective-permute-start.14
  84.2 4.6 collective-permute-done.7
  88.8 1.0 constant_dynamic-update-slice_fusion.31
  89.8 1.0 constant_dynamic-update-slice_fusion.30
  90.8 1.0 constant_dynamic-update-slice_fusion.29
  91.9 1.0 constant_dynamic-update-slice_fusion.28
  92.9 1.0 constant_dynamic-update-slice_fusion.27
  93.9 1.0 constant_dynamic-update-slice_fusion.26
  95.0 1.0 constant_dynamic-update-slice_fusion.25
  96.0 1.0 constant_dynamic-update-slice_fusion.23
  97.1 1.0 constant_dynamic-update-slice_fusion.21
  98.1 1.0 constant_dynamic-update-slice_fusion.20
  99.1 1.0 constant_dynamic-update-slice_fusion.19
  100.2 1.0 constant_dynamic-update-slice_fusion.18
  101.2 1.0 constant_dynamic-update-slice_fusion.17
  102.3 1.0 constant_dynamic-update-slice_fusion.15
  103.3 1.0 constant_dynamic-update-slice_fusion.14
  104.8 1.0 constant_dynamic-update-slice_fusion.2
  105.8 1.0 constant_dynamic-update-slice_fusion.1
  106.9 1.9 fusion.15
  108.8 1.4 copy.24
  110.2 27.8 %all_to_all.37 = bf16[256,3,1024]{0,1,2:T(4,128)(2,1)S(1)} all-to-all(bf16[256,3,1024]{0,1,2:T(4,128)(2,1)S(1)} %copy.24), channel_id=1, replica_groups=mesh['span'=16,'seq'=2] {'seq'}, dimensions={2} | all-to-all | bytes 3145728 | tf_op jit(solution)/shard_map/all_to_all | solution.py:37
  138.0 3.1 copy.25
  141.1 3.7 all_to_all.30
  144.8 1.5 fusion.26
  146.3 1.3 multiply_reduce_fusion
  147.6 1.4 fusion.7
  149.0 2.4 divide_convert_fusion
  151.4 1.2 all_to_all.31
  152.6 0.9 copy.27
  153.4 3.5 all-to-all-start.1
  157.0 3.9 copy.30
  160.9 3.1 all-to-all-done.1
  164.0 0.8 fusion.28
  165.4 3.7 convolution_convert_fusion
  169.0 0.9 fusion.27
  169.9 1.2 copy.29
  171.2 10.3 %bitcast_reduce_fusion = (f32[1024,16]{0,1:T(8,128)}, f32[16,256,1024]{2,1,0:T(8,128)}) fusion(bf16[256,16,64]{0,2,1:T(8,128)(2,1)S(1)} %bitcast.56, bf16[1024,16,64]{0,2,1:T(8,128)(2,1)} %bitcast.53), kind=kOutput, calls=%fused_computation.1 | convolution fusion | flops 545243136 | bytes 19464192 | tf_op jit(solution)/shard_map/qhd,khd->qhk/dot_general | solution.py:75
  182.0 115.3 %all-reduce.4.cloned.1.call-done = f32[1024,16]{0,1:T(8,128)} async-done(((f32[1024,16]{0,1:T(8,128)}), f32[1024,16]{0,1:T(8,128)}) %all-reduce.4.cloned.1.call-update) | async-done | bytes 65552 | tf_op jit(solution)/shard_map/pmax | solution.py:79
  297.2 10.8 %fusion.3 = f32[16,64,1024]{2,1,0:T(8,128)} fusion(bf16[256,16,64]{0,2,1:T(8,128)(2,1)S(1)} %bitcast.59, f32[16,256,1024]{2,1,0:T(8,128)} %get-tuple-element.29, f32[1024,16]{0,1:T(8,128)} %all-reduce.4.cloned.1.call-done), kind=kOutput, calls=%fused_computation.5 | convolution fusion | flops 549453824 | bytes 21561344 | tf_op jit(solution)/shard_map/qhk,khd->qhd/dot_general | solution.py:82
  308.0 5.3 %copy.32 = f32[1024,1024]{1,0:T(8,128)} copy(f32[1024,1024]{0,1:T(8,128)} %bitcast.52) | data formatting | bytes 8388608 | tf_op jit(solution)/shard_map/reshape | solution.py:88
  313.3 9.3 %fusion.1 = f32[1024,16]{0,1:T(8,128)} fusion(f32[16,256,1024]{2,1,0:T(8,128)} %get-tuple-element.29, f32[1024,16]{0,1:T(8,128)S(1)} %copy-done.21), kind=kLoop, calls=%fused_computation.3 | loop fusion | flops 12566528 | bytes 16908288 | tf_op jit(solution)/shard_map/reduce_sum | solution.py:81
  322.7 144.6 %all-reduce.6.cloned.1.call-done = (f32[1024,16]{0,1:T(8,128)}, f32[1024,1024]{1,0:T(8,128)}) async-done(((f32[1024,16]{0,1:T(8,128)}, f32[1024,1024]{1,0:T(8,128)}), (f32[1024,16]{0,1:T(8,128)}, f32[1024,1024]{1,0:T(8,128)})) %all-reduce.6.cloned.1.call-update) | async-done | bytes 4259856 | tf_op jit(solution)/shard_map/psum | solution.py:90
  467.2 0.8 constant_dynamic-slice_fusion
  468.4 1.7 divide_convert_fusion.1
  (84 shorter events, 2.5 us)
Async XLA Ops:
  7.2 156.8 %copy-start = (bf16[1024,1024]{1,0:T(8,128)(2,1)S(1)}, bf16[1024,1024]{1,0:T(8,128)(2,1)}, u32[]{:S(2)}) copy-start(bf16[1024,1024]{1,0:T(8,128)(2,1)} %param.9) | copy-start | bytes 6291460
  7.2 97.4 %copy-start.1 = (bf16[64,3072]{1,0:T(8,128)(2,1)S(1)}, bf16[64,3072]{1,0:T(8,128)(2,1)}, u32[]{:S(2)}) copy-start(bf16[64,3072]{1,0:T(8,128)(2,1)} %param.8) | copy-start | bytes 1179652
  7.2 11.2 %collective-permute-start = (bf16[64,3072]{1,0:T(8,128)(2,1)}, bf16[64,3072]{1,0:T(8,128)(2,1)S(1)}, u32[]{:S(2)}, u32[]{:S(2)}) collective-permute-start(bf16[64,3072]{1,0:T(8,128)(2,1)} %param.8), channel_id=1, source_target_pairs={{0,2},{2,4},{4,6},{6,8},{8,10},{10,12},{12,14},{14,16},{16,18},{18... | collective-permute-start | bytes 1179656 | tf_op jit(solution)/shard_map/ppermute | solution.py:17
  18.4 10.0 %collective-permute-start.1 = (bf16[64,3072]{1,0:T(8,128)(2,1)S(1)}, bf16[64,3072]{1,0:T(8,128)(2,1)S(1)}, u32[]{:S(2)}, u32[]{:S(2)}) collective-permute-start(bf16[64,3072]{1,0:T(8,128)(2,1)S(1)} %collective-permute-done), channel_id=1, source_target_pairs={{0,2},{2,4},{4,6},{6,8},{8,10},{10,12},{12,14},{14,16},{16,18},{18... | collective-permute-start | bytes 1179656 | tf_op jit(solution)/shard_map/ppermute | solution.py:17
  18.4 10.1 %collective-permute-start.8 = (bf16[64,3072]{1,0:T(8,128)(2,1)}, bf16[64,3072]{1,0:T(8,128)(2,1)S(1)}, u32[]{:S(2)}, u32[]{:S(2)}) collective-permute-start(bf16[64,3072]{1,0:T(8,128)(2,1)} %param.8), channel_id=1, source_target_pairs={{0,30},{2,0},{4,2},{6,4},{8,6},{10,8},{12,10},{14,12},{16,14},{18,... | collective-permute-start | bytes 1179656 | tf_op jit(solution)/shard_map/ppermute | solution.py:19
  28.4 10.0 %copy-start.2 = (bf16[64,3072]{1,0:T(8,128)(2,1)}, bf16[64,3072]{1,0:T(8,128)(2,1)S(1)}, u32[]{:S(2)}) copy-start(bf16[64,3072]{1,0:T(8,128)(2,1)S(1)} %collective-permute-done.1) | copy-start | bytes 1179652
  28.4 10.0 %collective-permute-start.2 = (bf16[64,3072]{1,0:T(8,128)(2,1)S(1)}, bf16[64,3072]{1,0:T(8,128)(2,1)S(1)}, u32[]{:S(2)}, u32[]{:S(2)}) collective-permute-start(bf16[64,3072]{1,0:T(8,128)(2,1)S(1)} %collective-permute-done.1), channel_id=1, source_target_pairs={{0,2},{2,4},{4,6},{6,8},{8,10},{10,12},{12,14},{14,16},{16,18},{18... | collective-permute-start | bytes 1179656 | tf_op jit(solution)/shard_map/ppermute | solution.py:17
  28.4 10.0 %collective-permute-start.9 = (bf16[64,3072]{1,0:T(8,128)(2,1)S(1)}, bf16[64,3072]{1,0:T(8,128)(2,1)S(1)}, u32[]{:S(2)}, u32[]{:S(2)}) collective-permute-start(bf16[64,3072]{1,0:T(8,128)(2,1)S(1)} %collective-permute-done.8), channel_id=1, source_target_pairs={{0,30},{2,0},{4,2},{6,4},{8,6},{10,8},{12,10},{14,12},{16,14},{18,... | collective-permute-start | bytes 1179656 | tf_op jit(solution)/shard_map/ppermute | solution.py:19
  38.4 10.4 %copy-start.6 = (bf16[64,3072]{1,0:T(8,128)(2,1)}, bf16[64,3072]{1,0:T(8,128)(2,1)S(1)}, u32[]{:S(2)}) copy-start(bf16[64,3072]{1,0:T(8,128)(2,1)S(1)} %collective-permute-done.2) | copy-start | bytes 1179652
  38.4 10.0 %collective-permute-start.3 = (bf16[64,3072]{1,0:T(8,128)(2,1)S(1)}, bf16[64,3072]{1,0:T(8,128)(2,1)S(1)}, u32[]{:S(2)}, u32[]{:S(2)}) collective-permute-start(bf16[64,3072]{1,0:T(8,128)(2,1)S(1)} %collective-permute-done.2), channel_id=1, source_target_pairs={{0,2},{2,4},{4,6},{6,8},{8,10},{10,12},{12,14},{14,16},{16,18},{18... | collective-permute-start | bytes 1179656 | tf_op jit(solution)/shard_map/ppermute | solution.py:17
  38.4 4.6 copy-start.4
  38.4 10.4 %collective-permute-start.10 = (bf16[64,3072]{1,0:T(8,128)(2,1)S(1)}, bf16[64,3072]{1,0:T(8,128)(2,1)S(1)}, u32[]{:S(2)}, u32[]{:S(2)}) collective-permute-start(bf16[64,3072]{1,0:T(8,128)(2,1)S(1)} %collective-permute-done.9), channel_id=1, source_target_pairs={{0,30},{2,0},{4,2},{6,4},{8,6},{10,8},{12,10},{14,12},{16,14},{18,... | collective-permute-start | bytes 1179656 | tf_op jit(solution)/shard_map/ppermute | solution.py:19
  48.4 20.7 %copy-start.12 = (bf16[64,3072]{1,0:T(8,128)(2,1)}, bf16[64,3072]{1,0:T(8,128)(2,1)S(1)}, u32[]{:S(2)}) copy-start(bf16[64,3072]{1,0:T(8,128)(2,1)S(1)} %collective-permute-done.3) | copy-start | bytes 1179652
  48.4 10.0 %collective-permute-start.4 = (bf16[64,3072]{1,0:T(8,128)(2,1)S(1)}, bf16[64,3072]{1,0:T(8,128)(2,1)S(1)}, u32[]{:S(2)}, u32[]{:S(2)}) collective-permute-start(bf16[64,3072]{1,0:T(8,128)(2,1)S(1)} %collective-permute-done.3), channel_id=1, source_target_pairs={{0,2},{2,4},{4,6},{6,8},{8,10},{10,12},{12,14},{14,16},{16,18},{18... | collective-permute-start | bytes 1179656 | tf_op jit(solution)/shard_map/ppermute | solution.py:17
  48.8 4.2 copy-start.8
  48.8 10.7 %collective-permute-start.11 = (bf16[64,3072]{1,0:T(8,128)(2,1)S(1)}, bf16[64,3072]{1,0:T(8,128)(2,1)S(1)}, u32[]{:S(2)}, u32[]{:S(2)}) collective-permute-start(bf16[64,3072]{1,0:T(8,128)(2,1)S(1)} %collective-permute-done.10), channel_id=1, source_target_pairs={{0,30},{2,0},{4,2},{6,4},{8,6},{10,8},{12,10},{14,12},{16,14},{18,... | collective-permute-start | bytes 1179656 | tf_op jit(solution)/shard_map/ppermute | solution.py:19
  58.4 15.5 %copy-start.14 = (bf16[64,3072]{1,0:T(8,128)(2,1)}, bf16[64,3072]{1,0:T(8,128)(2,1)S(1)}, u32[]{:S(2)}) copy-start(bf16[64,3072]{1,0:T(8,128)(2,1)S(1)} %collective-permute-done.4) | copy-start | bytes 1179652
  58.4 10.0 %collective-permute-start.5 = (bf16[64,3072]{1,0:T(8,128)(2,1)S(1)}, bf16[64,3072]{1,0:T(8,128)(2,1)S(1)}, u32[]{:S(2)}, u32[]{:S(2)}) collective-permute-start(bf16[64,3072]{1,0:T(8,128)(2,1)S(1)} %collective-permute-done.4), channel_id=1, source_target_pairs={{0,2},{2,4},{4,6},{6,8},{8,10},{10,12},{12,14},{14,16},{16,18},{18... | collective-permute-start | bytes 1179656 | tf_op jit(solution)/shard_map/ppermute | solution.py:17
  59.5 0.8 copy-start.10
  60.3 8.8 %collective-permute-start.12 = (bf16[64,3072]{1,0:T(8,128)(2,1)S(1)}, bf16[64,3072]{1,0:T(8,128)(2,1)}, u32[]{:S(2)}, u32[]{:S(2)}) collective-permute-start(bf16[64,3072]{1,0:T(8,128)(2,1)S(1)} %collective-permute-done.11), channel_id=1, source_target_pairs={{0,30},{2,0},{4,2},{6,4},{8,6},{10,8},{12,10},{14,12},{16,14},{18,... | collective-permute-start | bytes 1179656 | tf_op jit(solution)/shard_map/ppermute | solution.py:19
  68.4 10.1 %copy-start.16 = (bf16[64,3072]{1,0:T(8,128)(2,1)}, bf16[64,3072]{1,0:T(8,128)(2,1)S(1)}, u32[]{:S(2)}) copy-start(bf16[64,3072]{1,0:T(8,128)(2,1)S(1)} %collective-permute-done.5) | copy-start | bytes 1179652
  68.4 10.1 %collective-permute-start.6 = (bf16[64,3072]{1,0:T(8,128)(2,1)S(1)}, bf16[64,3072]{1,0:T(8,128)(2,1)}, u32[]{:S(2)}, u32[]{:S(2)}) collective-permute-start(bf16[64,3072]{1,0:T(8,128)(2,1)S(1)} %collective-permute-done.5), channel_id=1, source_target_pairs={{0,2},{2,4},{4,6},{6,8},{8,10},{10,12},{12,14},{14,16},{16,18},{18... | collective-permute-start | bytes 1179656 | tf_op jit(solution)/shard_map/ppermute | solution.py:17
  69.1 10.4 %collective-permute-start.13 = (bf16[64,3072]{1,0:T(8,128)(2,1)}, bf16[64,3072]{1,0:T(8,128)(2,1)}, u32[]{:S(2)}, u32[]{:S(2)}) collective-permute-start(bf16[64,3072]{1,0:T(8,128)(2,1)} %collective-permute-done.12), channel_id=1, source_target_pairs={{0,30},{2,0},{4,2},{6,4},{8,6},{10,8},{12,10},{14,12},{16,14},{18,... | collective-permute-start | bytes 1179656 | tf_op jit(solution)/shard_map/ppermute | solution.py:19
  78.5 10.3 %collective-permute-start.7 = (bf16[64,3072]{1,0:T(8,128)(2,1)}, bf16[64,3072]{1,0:T(8,128)(2,1)}, u32[]{:S(2)}, u32[]{:S(2)}) collective-permute-start(bf16[64,3072]{1,0:T(8,128)(2,1)} %collective-permute-done.6), channel_id=1, source_target_pairs={{0,2},{2,4},{4,6},{6,8},{8,10},{10,12},{12,14},{14,16},{16,18},{18... | collective-permute-start | bytes 1179656 | tf_op jit(solution)/shard_map/ppermute | solution.py:17
  79.1 25.2 %copy-start.17 = (bf16[64,3072]{1,0:T(8,128)(2,1)S(1)}, bf16[64,3072]{1,0:T(8,128)(2,1)}, u32[]{:S(2)}) copy-start(bf16[64,3072]{1,0:T(8,128)(2,1)} %copy-done.16) | copy-start | bytes 1179652
  79.1 25.3 %copy-start.15 = (bf16[64,3072]{1,0:T(8,128)(2,1)S(1)}, bf16[64,3072]{1,0:T(8,128)(2,1)}, u32[]{:S(2)}) copy-start(bf16[64,3072]{1,0:T(8,128)(2,1)} %copy-done.14) | copy-start | bytes 1179652
  79.1 25.3 %copy-start.13 = (bf16[64,3072]{1,0:T(8,128)(2,1)S(1)}, bf16[64,3072]{1,0:T(8,128)(2,1)}, u32[]{:S(2)}) copy-start(bf16[64,3072]{1,0:T(8,128)(2,1)} %copy-done.12) | copy-start | bytes 1179652
  79.1 25.4 %copy-start.7 = (bf16[64,3072]{1,0:T(8,128)(2,1)S(1)}, bf16[64,3072]{1,0:T(8,128)(2,1)}, u32[]{:S(2)}) copy-start(bf16[64,3072]{1,0:T(8,128)(2,1)} %copy-done.6) | copy-start | bytes 1179652
  79.1 25.4 %copy-start.3 = (bf16[64,3072]{1,0:T(8,128)(2,1)S(1)}, bf16[64,3072]{1,0:T(8,128)(2,1)}, u32[]{:S(2)}) copy-start(bf16[64,3072]{1,0:T(8,128)(2,1)} %copy-done.2) | copy-start | bytes 1179652
  79.1 25.6 %copy-start.5 = (bf16[64,3072]{1,0:T(8,128)(2,1)S(1)}, bf16[64,3072]{1,0:T(8,128)(2,1)}, u32[]{:S(2)}) copy-start(bf16[64,3072]{1,0:T(8,128)(2,1)} %copy-done.4) | copy-start | bytes 1179652
  79.1 25.6 %copy-start.9 = (bf16[64,3072]{1,0:T(8,128)(2,1)S(1)}, bf16[64,3072]{1,0:T(8,128)(2,1)}, u32[]{:S(2)}) copy-start(bf16[64,3072]{1,0:T(8,128)(2,1)} %copy-done.8) | copy-start | bytes 1179652
  79.1 25.6 %copy-start.11 = (bf16[64,3072]{1,0:T(8,128)(2,1)S(1)}, bf16[64,3072]{1,0:T(8,128)(2,1)}, u32[]{:S(2)}) copy-start(bf16[64,3072]{1,0:T(8,128)(2,1)} %copy-done.10) | copy-start | bytes 1179652
  79.1 27.8 %copy-start.18 = (bf16[256,1024]{1,0:T(8,128)(2,1)S(1)}, bf16[256,1024]{1,0:T(8,128)(2,1)}, u32[]{:S(2)}) copy-start(bf16[256,1024]{1,0:T(8,128)(2,1)} %param.7) | copy-start | bytes 1572868
  79.5 22.7 %collective-permute-start.14 = (bf16[64,3072]{1,0:T(8,128)(2,1)}, bf16[64,3072]{1,0:T(8,128)(2,1)S(1)}, u32[]{:S(2)}, u32[]{:S(2)}) collective-permute-start(bf16[64,3072]{1,0:T(8,128)(2,1)} %collective-permute-done.13), channel_id=1, source_target_pairs={{0,30},{2,0},{4,2},{6,4},{8,6},{10,8},{12,10},{14,12},{16,14},{18,... | collective-permute-start | bytes 1179656 | tf_op jit(solution)/shard_map/ppermute | solution.py:19
  147.6 16.4 %copy-start.19 = (bf16[256,1024]{1,0:T(8,128)(2,1)S(1)}, bf16[256,1024]{1,0:T(8,128)(2,1)}, u32[]{:S(2)}) copy-start(bf16[256,1024]{1,0:T(8,128)(2,1)} %param.7) | copy-start | bytes 1572868
  149.0 16.1 %copy-start.22 = (f32[1024]{0:T(1024)S(1)}, f32[1024]{0:T(1024)}, u32[]{:S(2)}) copy-start(f32[1024]{0:T(1024)} %param.12) | copy-start | bytes 12292
  149.0 16.1 %copy-start.23 = (f32[1024]{0:T(1024)S(1)}, f32[1024]{0:T(1024)}, u32[]{:S(2)}) copy-start(f32[1024]{0:T(1024)} %param.11) | copy-start | bytes 12292
  153.4 10.5 %all-to-all-start.1 = ((bf16[2,256,512]{1,2,0:T(8,128)(2,1)}), bf16[2,256,512]{1,2,0:T(8,128)(2,1)S(1)}, u32[]{:S(2)}, u32[]{:S(2)}) async-start(bf16[2,256,512]{1,2,0:T(8,128)(2,1)} %copy.27), calls=%async_computation.1 | async-start | bytes 1048576 | tf_op jit(solution)/shard_map/all_to_all | solution.py:64
  156.9 140.3 %all-reduce.4.cloned.1.call-start = ((), (), s32[]{:S(2)}) async-start(), calls=%async_computation.2 | async-start | bytes 131072 | tf_op jit(solution)/shard_map/pmax | solution.py:79
  165.3 4.6 copy-start.20
  181.5 285.7 %all-reduce.6.cloned.1.call-start = ((), (), s32[]{:S(2)}) async-start(), calls=%async_computation.3 | async-start | bytes 8519680 | tf_op jit(solution)/shard_map/psum | solution.py:90
  297.2 16.1 %copy-start.21 = (f32[1024,16]{0,1:T(8,128)S(1)}, f32[1024,16]{0,1:T(8,128)}, u32[]{:S(2)}) copy-start(f32[1024,16]{0,1:T(8,128)} %all-reduce.4.cloned.1.call-done) | copy-start | bytes 196612
Sparse Core Ops, SparseCore 0:
  181.6 115.5 all-reduce.3
  322.8 144.3 all-reduce.5
